TPU v7x, 512 devices: a whole 4x4x16 slice. The times are simulated.
512 devices in a mesh: wide: 64 (over y, z), narrow: 8 (over x, core).
Axes of the slice: x: 4, y: 4, z: 16, core: 2. Of those that a mesh axis runs over, the one named last changes fastest.
Arguments:
- integrals: bfloat16 [512, 6, 256, 1024], P(('wide', 'narrow')), may hold values from -1 to 1
- amplitudes: bfloat16 [512, 6, 256, 512], P(('wide', 'narrow')), may hold values from -6 to 6
- tile_count: int32 [512], P(('wide', 'narrow')), may hold values from 1 to 6, as said below
- row_orbitals: int32 [1024, 2], P(('wide', 'narrow')), may hold values from 0 to 575
- virtual_energy: float32 [576], replicated, may hold values from 0.2 to 3
- occupied_energy: float32 [512], replicated, may hold values from -3 to -0.8
- other_terms: float32 [1024, 512], P(('wide', 'narrow')), may hold values from -20 to 20
Outputs:
- update: float32 [1024, 512], P(('wide', 'narrow'))
- update_norm: float32 [], replicated
Inputs may be any that keep to these rules, and one draw needn't show every extreme that they name: A device's screened tiles are its first tile_count slots; some device holds 6 in every draw.
All inputs are finite; a program needn't handle non-finite values.
Results may differ from a plain program's by a relative error of at most 0.0003.
Values sent between devices are 32-bit elements; how exact they have to be, the bound alone decides.
A program may use at most 64 MiB of HBM per device.

v0:
```python
import jax
import jax.numpy as jnp
from jax import lax
from jax.sharding import PartitionSpec as P


def add_slots(tile_block, amp_rows, lower, upper, row_total, running):
    tile_len = tile_block.shape[1]

    def add_tile(slot_index, partial_value):
        tile_one = lax.dynamic_slice(tile_block, (slot_index, 0, 0), (1, tile_len, row_total))[0]
        amp_one = lax.dynamic_index_in_dim(amp_rows, slot_index, 0, keepdims=False)
        return partial_value + lax.dot_general(
            tile_one, amp_one, (((0,), (0,)), ((), ())), preferred_element_type=jnp.float32
        )

    return lax.fori_loop(lower, upper, add_tile, running)


def shards(
    integrals, amplitudes, tile_count, row_orbitals, virtual_energy, occupied_energy, other_terms
):
    tile_block = integrals[0]
    amp_rows = amplitudes[0]
    live_count = tile_count[0]
    rows_all = tile_block.shape[2]
    width = amp_rows.shape[2]
    zero_index = jnp.int32(0)
    row_total = lax.axis_size(("wide", "narrow")) * other_terms.shape[0]
    running = jnp.zeros((row_total, width), jnp.float32)
    ladder = lax.psum_scatter(
        add_slots(tile_block, amp_rows, zero_index, live_count, row_total, running),
        ("wide", "narrow"),
        scatter_dimension=0,
        tiled=True,
    )
    orbital_ids = lax.broadcasted_iota(jnp.int32, (1, virtual_energy.shape[0]), 1)
    energy_row = virtual_energy[None, :]
    first_energy = jnp.sum(jnp.where(row_orbitals[:, 0:1] == orbital_ids, energy_row, 0.0), axis=1)
    second_energy = jnp.sum(jnp.where(row_orbitals[:, 1:2] == orbital_ids, energy_row, 0.0), axis=1)
    denominator = occupied_energy[None, :] - (first_energy + second_energy)[:, None]
    update = (ladder + other_terms) / denominator
    square_total = lax.psum(jnp.sum(update * update), ("wide", "narrow"))
    update_norm = jnp.sqrt(square_total / (rows_all * width))
    return (update, update_norm)


def solution(mesh):
    in_specs = (
        P(("wide", "narrow"), None, None, None),
        P(("wide", "narrow"), None, None, None),
        P(("wide", "narrow")),
        P(("wide", "narrow"), None),
        P(),
        P(),
        P(("wide", "narrow"), None),
    )
    out_specs = (P(("wide", "narrow"), None), P())
    return jax.shard_map(shards, mesh=mesh, in_specs=in_specs, out_specs=out_specs, check_vma=False)
```

profile of v0, /device:TPU:1, one launch (start us, length us, event | category | flops | bytes accessed | tf_op | source)
XLA Modules:
  0.0 617.5 jit_solution(16076494832805641768)
XLA Ops:
  7.2 0.0 all-reduce.3.cloned.1.call-start
  7.2 0.2 broadcast_in_dim.22
  7.5 2.9 while.10
  8.1 1.6 convolution_add_fusion.2
  10.4 0.0 copy-start
  10.4 0.0 copy-start.2
  10.4 0.0 copy-start.1
  10.4 0.0 copy-start.3
  10.4 0.0 copy-start.4
  10.4 1.2 copy-done
  11.7 0.0 all-reduce.3.cloned.1.call-update
  11.7 0.0 copy-done.2
  11.7 0.2 slice_reduce_fusion
  11.9 0.0 copy-done.1
  11.9 0.2 fusion.6
  12.2 491.5 %all-reduce.3.cloned.1.call-done = f32[1024,512]{1,0:T(8,128)} async-done(((f32[1024,512]{1,0:T(8,128)}), f32[1024,512]{1,0:T(8,128)}) %all-reduce.3.cloned.1.call-update) | async-done | bytes 2097168
  503.7 0.0 copy-done.3
  503.7 0.0 copy-done.4
  503.7 2.0 multiply_reduce_fusion
  505.7 103.2 %psum.7 = f32[]{:T(128)} all-reduce(f32[]{:T(128)} %get-tuple-element.45), channel_id=1, replica_groups=mesh['wide'=64,'narrow'=8] {'wide','narrow'}, use_global_device_ids=true, to_apply=%region_6.7 | all-reduce | flops 1 | bytes 8 | tf_op jit(solution)/shard_map/psum | solution.py:43
  (1 shorter events, 0.0 us)
Async XLA Ops:
  7.2 496.5 %all-reduce.3.cloned.1.call-start = ((), (), s32[]{:S(2)}) async-start(), calls=%async_computation | async-start | bytes 4194304
  10.4 1.3 copy-start
  10.4 1.3 copy-start.2
  10.4 1.5 copy-start.1
  10.4 493.3 %copy-start.3 = (f32[2,512]{1,0:T(2,128)S(1)}, f32[2,512]{1,0:T(2,128)}, u32[]{:S(2)}) copy-start(f32[2,512]{1,0:T(2,128)} %param.15) | copy-start | bytes 12292
  10.4 493.3 %copy-start.4 = (f32[512]{0:T(512)S(1)}, f32[512]{0:T(512)}, u32[]{:S(2)}) copy-start(f32[512]{0:T(512)} %param.14) | copy-start | bytes 6148
Sparse Core Ops, SparseCore 0:
  13.3 490.3 all-reduce.2
where the time goes:
time: 618 us
  waiting for transfers between devices  492 us (80%)
  blocking collectives  103 us (17%)
  between operations  15.9 us (3%)
    unnamed x2, waiting for transfers between devices  492 us
    psum x1, blocking collectives, shards(): square_total = lax.psum(jnp.sum(update * update), ('wide', 'narrow'))  103 us
  transfers between devices with their start and end apart: 1, of which 1 were waited for; matrix products, arithmetic and copies ran while one was open for 0% of the time, Pallas kernels for 0%

commit v1 on v0

v1 whole, which is shorter than its diff:
```python
import functools

import jax
import jax.numpy as jnp
from jax import lax
from jax.experimental import pallas as pl
from jax.experimental.pallas import tpu as pltpu
from jax.sharding import PartitionSpec as P

MESH = pl.DeviceIdType.MESH
NX, NY, NZ = 4, 4, 16
SLOTS, TILE = 6, 256
HOPS = (2, 1, 3)
Z_HOPS = (8, 7, 9, 6, 10, 5, 11, 4, 12, 3, 13, 2, 14, 1, 15)


def wait_bytes(ref, sem):
    pltpu.make_async_copy(ref, ref, sem).wait()


def kernel(
    integrals, amplitudes, count, orbitals, virtual, occupied, other,
    out, norm,
    amp, tiles, mine, theirs, core_in,
    x_in, y_in, y_sum, y2_in, x_sum, x2_in, final, z_in,
    early_out, early_in, late_out, late_in, za, zb,
    amp_sem, tile_sem, core_send, core_recv, x_send, x_recv, y_send, y_recv,
    y2_send, y2_recv, x2_send, x2_recv, z_send, z_recv,
    early_send, early_recv, late_send, late_recv, za_send, za_recv, zb_send, zb_recv,
):
    wide, narrow = lax.axis_index("wide"), lax.axis_index("narrow")
    y, z = wide // NZ, wide % NZ
    x, c = narrow // 2, narrow % 2

    def at(x=x, y=y, z=z, c=c):
        return (y * NZ + z, x * 2 + c)

    def send(src, dst, send_sem, recv_sem, device):
        pltpu.make_async_remote_copy(
            src_ref=src, dst_ref=dst, send_sem=send_sem, recv_sem=recv_sem,
            device_id=device, device_id_type=MESH,
        ).start()

    rank = (y * NX + x) * 2 + c
    order = [(y + hop) % NY for hop in HOPS] + [y]

    for half, cc in enumerate((1 - c, c)):
        pltpu.make_async_copy(
            amplitudes.at[0, :, :, pl.ds(pl.multiple_of(cc * 256, 256), 256)],
            amp.at[half], amp_sem.at[half],
        ).start()
    for k in range(4):
        pltpu.make_async_copy(
            integrals.at[0, :, :, pl.ds(pl.multiple_of(order[k] * 256, 256), 256)],
            tiles.at[k], tile_sem.at[k],
        ).start()

    barrier = pltpu.get_barrier_semaphore()

    def greet(device):
        pl.semaphore_signal(barrier, inc=1, device_id=device, device_id_type=MESH)

    for hop in range(1, NZ):
        greet(at(z=(z + hop) % NZ))
    for hop in range(1, 2 * NX * NY):
        r = (rank + hop) % (2 * NX * NY)
        greet(at(x=(r // 2) % NX, y=r // (2 * NX), c=r % 2))

    pair = x + 1 - 2 * (x % 2)
    place = 2 * (x % 2) + c
    column = 2 * c + x % 2
    partners = ((pair, 1 - c), (pair, c), (x, 1 - c))
    for i in range(2):
        level = virtual[orbitals[i, 0]] + virtual[orbitals[i, 1]]
        denominator = occupied[...] - level
        for t in range(4):
            early_out[t, i : i + 1, :] = other[i : i + 1, t * 128 : (t + 1) * 128]
            early_out[t, 2 + i : 3 + i, :] = denominator[:, t * 128 : (t + 1) * 128]

    live = count[0]
    for half in range(2):
        wait_bytes(amp.at[half], amp_sem.at[half])
        for s in range(SLOTS):
            keep = jnp.full((TILE, 256), live, jnp.int32) > s
            value = amp[half, s]
            amp[half, s] = jnp.where(keep, value, jnp.zeros_like(value))

    def multiply(k, half, dst):
        product = lax.dot_general(
            tiles[k].reshape(SLOTS * TILE, 256), amp[half].reshape(SLOTS * TILE, 256),
            (((0,), (0,)), ((), ())), preferred_element_type=jnp.float32,
        ).reshape(NZ, 2, 8, 256)
        for xx in range(NX):
            dst[k, xx] = product[:, xx // 2, :, (xx % 2) * 128 : (xx % 2 + 1) * 128]

    def core_done(k):
        wait_bytes(core_in.at[k], core_recv.at[k])
        mine[k] = mine[k] + core_in[k]
        for n, hop in enumerate(HOPS):
            xt = (x + hop) % NX
            send(mine.at[k, xt, pl.ds(0, 8)], x_in.at[k, n], x_send, x_recv.at[k], at(x=xt))
        if k < 3:
            send(mine.at[k, :, pl.ds(8, 8)], y_in.at[k], y_send, y_recv.at[k], at(y=order[k]))

    for k in range(4):
        wait_bytes(tiles.at[k], tile_sem.at[k])
        multiply(k, 0, theirs)
        if k == 0:
            pl.semaphore_wait(barrier, (NZ - 1) + (2 * NX * NY - 1))
            for xp, cp in partners:
                send(early_out.at[2 * cp + xp % 2], early_in.at[place], early_send, early_recv, at(x=xp, c=cp))
            early_in[place] = early_out[column]
        send(theirs.at[k], core_in.at[k], core_send, core_recv.at[k], at(c=1 - c))
        multiply(k, 1, mine)
        if k > 0:
            core_done(k - 1)
    core_done(3)

    for k in range(4):
        wait_bytes(x_in.at[k], x_recv.at[k])
        total = mine[k, x, 0:8] + x_in[k, 0] + x_in[k, 1] + x_in[k, 2]
        if k < 3:
            y_sum[k] = total
            send(y_sum.at[k], y2_in.at[k], y2_send, y2_recv, at(y=order[k]))
        else:
            final[0:8] = total
    for k in range(3):
        wait_bytes(y_in.at[k], y_recv.at[k])
    x_sum[...] = mine[3, :, 8:16] + y_in[0] + y_in[1] + y_in[2]
    for n, hop in enumerate(HOPS):
        xt = (x + hop) % NX
        send(x_sum.at[xt], x2_in.at[n], x2_send, x2_recv, at(x=xt))
    wait_bytes(y2_in, y2_recv)
    final[0:8] = final[0:8] + y2_in[0] + y2_in[1] + y2_in[2]
    wait_bytes(x2_in, x2_recv)
    final[8:16] = x_sum[x] + x2_in[0] + x2_in[1] + x2_in[2]

    for n, hop in enumerate(Z_HOPS):
        zt = (z + hop) % NZ
        send(final.at[zt], z_in.at[n], z_send, z_recv, at(z=zt))
    wait_bytes(early_in.at[pl.ds(0, 3)], early_recv)
    wait_bytes(z_in, z_recv)
    ladder = final[z] + jnp.sum(z_in[...], axis=0)
    other_tile = jnp.concatenate([early_in[g, 0:2] for g in range(4)], axis=0)
    denominator_tile = jnp.concatenate([early_in[g, 2:4] for g in range(4)], axis=0)
    update = (ladder + other_tile) / denominator_tile

    za[z] = jnp.sum(update * update, axis=0, keepdims=True)
    for n, hop in enumerate(Z_HOPS):
        zt = (z + hop) % NZ
        send(za.at[z], za.at[z], za_send, za_recv, at(z=zt))
    for g in range(4):
        late_out[g] = update[2 * g : 2 * g + 2]
    for xp, cp in partners:
        send(late_out.at[2 * (xp % 2) + cp], late_in.at[column], late_send, late_recv, at(x=xp, c=cp))
    late_in[column] = late_out[place]
    wait_bytes(za.at[pl.ds(0, NZ - 1)], za_recv)
    zb[rank] = jnp.sum(za[...], axis=0)
    for hop in range(1, 2 * NX * NY):
        r = (rank + hop) % (2 * NX * NY)
        send(zb.at[rank], zb.at[rank], zb_send, zb_recv, at(x=(r // 2) % NX, y=r // (2 * NX), c=r % 2))
    wait_bytes(late_in.at[pl.ds(0, 3)], late_recv)
    for t in range(4):
        out[:, t * 128 : (t + 1) * 128] = late_in[t]
    wait_bytes(zb.at[pl.ds(0, 2 * NX * NY - 1)], zb_recv)
    squares = jnp.sum(jnp.sum(zb[...], axis=0), axis=1, keepdims=True)
    norm[...] = jnp.sqrt(squares / (NX * NY * NZ * 2 * 2 * 512))

    wait_bytes(core_in, core_send)
    wait_bytes(x_in, x_send)
    wait_bytes(y_in, y_send)
    wait_bytes(y2_in, y2_send)
    wait_bytes(x2_in, x2_send)
    wait_bytes(z_in, z_send)
    wait_bytes(early_in.at[pl.ds(0, 3)], early_send)
    wait_bytes(late_in.at[pl.ds(0, 3)], late_send)
    wait_bytes(za.at[pl.ds(0, NZ - 1)], za_send)
    wait_bytes(zb.at[pl.ds(0, 2 * NX * NY - 1)], zb_send)


def shards(
    integrals, amplitudes, tile_count, row_orbitals, virtual_energy, occupied_energy, other_terms
):
    f32 = jnp.float32
    vmem = pl.BlockSpec(memory_space=pltpu.VMEM)
    smem = pl.BlockSpec(memory_space=pltpu.SMEM)
    hbm = pl.BlockSpec(memory_space=pl.ANY)
    dma = pltpu.SemaphoreType.DMA
    update, norm = pl.pallas_call(
        kernel,
        out_shape=(
            jax.ShapeDtypeStruct(other_terms.shape, f32),
            jax.ShapeDtypeStruct((1, 1), f32),
        ),
        in_specs=[hbm, hbm, smem, smem, smem, vmem, vmem],
        out_specs=(vmem, vmem),
        scratch_shapes=[
            pltpu.VMEM((2, SLOTS, TILE, 256), jnp.bfloat16),
            pltpu.VMEM((4, SLOTS, TILE, 256), jnp.bfloat16),
            pltpu.VMEM((4, NX, NZ, 8, 128), f32),
            pltpu.VMEM((4, NX, NZ, 8, 128), f32),
            pltpu.VMEM((4, NX, NZ, 8, 128), f32),
            pltpu.VMEM((4, 3, 8, 8, 128), f32),
            pltpu.VMEM((3, NX, 8, 8, 128), f32),
            pltpu.VMEM((3, 8, 8, 128), f32),
            pltpu.VMEM((3, 8, 8, 128), f32),
            pltpu.VMEM((NX, 8, 8, 128), f32),
            pltpu.VMEM((3, 8, 8, 128), f32),
            pltpu.VMEM((NZ, 8, 128), f32),
            pltpu.VMEM((NZ - 1, 8, 128), f32),
            pltpu.VMEM((4, 4, 128), f32),
            pltpu.VMEM((4, 4, 128), f32),
            pltpu.VMEM((4, 2, 128), f32),
            pltpu.VMEM((4, 2, 128), f32),
            pltpu.VMEM((NZ, 1, 128), f32),
            pltpu.VMEM((2 * NX * NY, 1, 128), f32),
            dma((2,)), dma((4,)), dma, dma((4,)), dma, dma((4,)), dma, dma((3,)),
            dma, dma, dma, dma, dma, dma,
            dma, dma, dma, dma, dma, dma, dma, dma,
        ],
        compiler_params=pltpu.CompilerParams(
            collective_id=0, has_side_effects=True, vmem_limit_bytes=32 << 20
        ),
    )(
        integrals, amplitudes, tile_count, row_orbitals, virtual_energy,
        occupied_energy[None, :], other_terms,
    )
    return (update, norm[0, 0])


def solution(mesh):
    in_specs = (
        P(("wide", "narrow"), None, None, None),
        P(("wide", "narrow"), None, None, None),
        P(("wide", "narrow")),
        P(("wide", "narrow"), None),
        P(),
        P(),
        P(("wide", "narrow"), None),
    )
    out_specs = (P(("wide", "narrow"), None), P())
    return jax.shard_map(shards, mesh=mesh, in_specs=in_specs, out_specs=out_specs, check_vma=False)
```

time: 618 us -> 62.4 us (0.10)
  waiting for transfers between devices: 492 us -> 0 us
  blocking collectives: 103 us -> 0 us
  Pallas kernels: 0 us -> 52.4 us
  between operations: 15.9 us -> 3.12 us
    unnamed x2 -> x0, waiting for transfers between devices: 492 us -> none
    psum x1 -> x0, blocking collectives: 103 us -> none  [shards(): square_total = lax.psum(jnp.sum(update * update), ('wide', 'narrow'))]
    pallas_call x0 -> x1, Pallas kernels: none -> 52.4 us  [shards(): pl.pallas_call(kernel, out_shape=(jax.ShapeDtypeStruct(other_terms.shape,...]
  transfers between devices with their start and end apart: 1 -> 0, of which waited for: 1 -> 0; matrix products, arithmetic and copies ran while one was open for 0% -> 0% of each run, Pallas kernels for 0% -> 0%
where the time goes in v1:
time: 62.4 us; the launch traced here: 62.1 us
  Pallas kernels  52.4 us (84%)
  local copies, waits for them, and re-layouts  6.62 us (11%)
  between operations  3.12 us (5%)
    pallas_call x1, Pallas kernels, shards(): pl.pallas_call(kernel, out_shape=(jax.ShapeDtypeStruct(other_terms.shape,...  52.4 us
    unnamed x13, local copies, waits for them, and re-layouts  6.62 us

profile of v1, /device:TPU:1, one launch (start us, length us, event | category | flops | bytes accessed | tf_op | source)
XLA Modules:
  0.0 62.1 jit_solution(4541045548395995321)
XLA Ops:
  1.3 0.0 copy-start
  1.3 1.9 %copy-done = bf16[1,6,256,1024]{3,2,1,0:T(8,128)(2,1)S(1)} copy-done((bf16[1,6,256,1024]{3,2,1,0:T(8,128)(2,1)S(1)}, bf16[1,6,256,1024]{3,2,1,0:T(8,128)(2,1)}, u32[]{:S(2)}) %copy-start) | copy-done | bytes 3145752
  3.2 0.0 copy-start.1
  3.2 1.4 %copy-done.1 = bf16[1,6,256,512]{3,2,1,0:T(8,128)(2,1)S(1)} copy-done((bf16[1,6,256,512]{3,2,1,0:T(8,128)(2,1)S(1)}, bf16[1,6,256,512]{3,2,1,0:T(8,128)(2,1)}, u32[]{:S(2)}) %copy-start.1) | copy-done | bytes 1572888
  4.6 0.0 copy-start.2
  4.6 0.7 %copy-done.2 = f32[576]{0:T(1024)S(1)} copy-done((f32[576]{0:T(1024)S(1)}, f32[576]{0:T(1024)}, u32[]{:S(2)}) %copy-start.2) | copy-done | bytes 2328
  5.3 0.0 copy-start.3
  5.3 0.7 %copy-done.3 = f32[2,512]{1,0:T(2,128)S(1)} copy-done((f32[2,512]{1,0:T(2,128)S(1)}, f32[2,512]{1,0:T(2,128)}, u32[]{:S(2)}) %copy-start.3) | copy-done | bytes 4120
  6.0 0.0 copy-start.4
  6.0 0.7 %copy-done.4 = f32[512]{0:T(512)S(1)} copy-done((f32[512]{0:T(512)S(1)}, f32[512]{0:T(512)}, u32[]{:S(2)}) %copy-start.4) | copy-done | bytes 2072
  6.6 0.0 copy-start.5
  6.6 0.7 %copy-done.5 = s32[2,2]{1,0:T(2,128)S(1)} copy-done((s32[2,2]{1,0:T(2,128)S(1)}, s32[2,2]{1,0:T(2,128)}, u32[]{:S(2)}) %copy-start.5) | copy-done | bytes 40
  7.3 52.4 %shard_map.86 = (f32[2,512]{1,0:T(2,128)S(1)}, f32[1,1]{1,0:T(1,128)}) custom-call(bf16[1,6,256,1024]{3,2,1,0:T(8,128)(2,1)S(1)} %copy-done, bf16[1,6,256,512]{3,2,1,0:T(8,128)(2,1)S(1)} %copy-done.1, s32[1]{0:T(128)S(6)} %copy.11.count, s32[2,2]{1,0:T(2,128)S(1)} %copy-done.5, f32[576]{0:T(1024)S(1)} %copy-done.2, f32[1,512]{1,0:T(1,128)S(1)} %bitcast.2, ...), custom_call_target="tpu_custom_call" | custom-call | tf_op jit(solution)/shard_map/pallas_call | solution.py:189
  59.7 0.6 copy.12
Async XLA Ops:
  1.3 1.9 %copy-start = (bf16[1,6,256,1024]{3,2,1,0:T(8,128)(2,1)S(1)}, bf16[1,6,256,1024]{3,2,1,0:T(8,128)(2,1)}, u32[]{:S(2)}) copy-start(bf16[1,6,256,1024]{3,2,1,0:T(8,128)(2,1)} %integrals.1) | copy-start | bytes 9437188
  3.2 1.4 %copy-start.1 = (bf16[1,6,256,512]{3,2,1,0:T(8,128)(2,1)S(1)}, bf16[1,6,256,512]{3,2,1,0:T(8,128)(2,1)}, u32[]{:S(2)}) copy-start(bf16[1,6,256,512]{3,2,1,0:T(8,128)(2,1)} %amplitudes.1) | copy-start | bytes 4718596
  4.6 0.7 %copy-start.2 = (f32[576]{0:T(1024)S(1)}, f32[576]{0:T(1024)}, u32[]{:S(2)}) copy-start(f32[576]{0:T(1024)} %virtual.1) | copy-start | bytes 6916
  5.3 0.7 %copy-start.3 = (f32[2,512]{1,0:T(2,128)S(1)}, f32[2,512]{1,0:T(2,128)}, u32[]{:S(2)}) copy-start(f32[2,512]{1,0:T(2,128)} %other.1) | copy-start | bytes 12292
  6.0 0.7 %copy-start.4 = (f32[512]{0:T(512)S(1)}, f32[512]{0:T(512)}, u32[]{:S(2)}) copy-start(f32[512]{0:T(512)} %param.12) | copy-start | bytes 6148
  6.6 0.7 %copy-start.5 = (s32[2,2]{1,0:T(2,128)S(1)}, s32[2,2]{1,0:T(2,128)}, u32[]{:S(2)}) copy-start(s32[2,2]{1,0:T(2,128)} %orbitals.1) | copy-start | bytes 52
